TPU v7x, 512 devices: a whole 4x8x8 slice. The times are simulated.
512 devices in a mesh: freq: 32 (over z, x_lo, core), tm: 16 (over x_hi, y).
Axes of the slice: x: 4 (x_hi: 2, x_lo: 2; x = x_hi * 2 + x_lo), y: 8, z: 8, core: 2. Of those that a mesh axis runs over, the one named last changes fastest.
Arguments:
- observed: bfloat16 [32, 16, 2, 512, 512], P('freq', 'tm'), may hold values from -6 to 6
- source_beams: bfloat16 [32, 16, 2, 256, 512], P('freq', 'tm'), may hold values from -1.1953125 to 1.1953125
- source_order: int32 [256], replicated, may hold values from 0 to 255, each once
- initial_gains: float32 [32, 2, 32, 512], P('freq'), may hold values from -2 to 2, as said below
- blending: float32 [32, 32], replicated, may hold values from 0 to 1, as said below
Outputs:
- residual: bfloat16 [32, 16, 2, 512, 512], P('freq', 'tm')
- smoothed_gains: float32 [32, 2, 32, 512], P('freq', None, 'tm')
Inputs may be any that keep to these rules, and one draw needn't show every extreme that they name: source_order holds every number of 0 to 255 once. Every row of blending is positive and sums to one. `initial_gains`: every complex gain has a magnitude between 0.5 and 2.
All inputs are finite; a program needn't handle non-finite values.
Results may differ from a plain program's by a relative error of at most 0.0034.
Values sent between devices are 32-bit elements; how exact they have to be, the bound alone decides.
No kernel may reach another device: no remote copies, remote signals or barrier semaphores. Data moves between devices by JAX's collectives and lax.ppermute only.
A program may use at most 64 MiB of HBM per device.

v0:
```python
import jax
import jax.numpy as jnp
from jax import lax
from jax.sharding import PartitionSpec as P

S = 512
K = 32
P_SIZE = 8


def apply_gains(gains, beams):
    real_part = gains[0][:, None, :] * beams[0] - gains[1][:, None, :] * beams[1]
    imag_part = gains[0][:, None, :] * beams[1] + gains[1][:, None, :] * beams[0]
    return jnp.stack([real_part, imag_part]).astype(jnp.bfloat16)


def predict(rounded):
    flat = rounded.reshape(2, rounded.shape[1] * rounded.shape[2], rounded.shape[3])
    joined = flat.reshape(2 * flat.shape[1], flat.shape[2])
    turned = jnp.concatenate([flat[1], -flat[0]], axis=0)
    stacked = jnp.stack([joined, turned])
    return lax.dot_general(
        stacked, joined, (((1,), (0,)), ((), ())), preferred_element_type=jnp.float32
    )


def update(totals, gains):
    denominator = totals[:, 2]
    ratio = jnp.stack([totals[:, 0], totals[:, 1]]) / denominator[None]
    return 0.5 * (ratio + gains)


def local(observed, source_beams, source_order, initial_gains, blending):
    observed_block = observed[0, 0]
    beam_block = source_beams[0, 0]
    start_gains = initial_gains[0]
    highest = lax.Precision.HIGHEST
    beam_float = (
        jnp.take(beam_block, source_order, axis=1).reshape(2, K, P_SIZE, S).astype(jnp.float32)
    )
    seeded = apply_gains(start_gains, beam_float)
    misfit = (observed_block.astype(jnp.float32) - predict(seeded)).astype(jnp.bfloat16)
    seeded_flat = seeded.reshape(2, K * P_SIZE, S)
    owned = K // lax.axis_size("tm")
    stacked = jnp.stack(
        [jnp.stack([seeded_flat[0], -seeded_flat[1]]), jnp.stack([seeded_flat[1], seeded_flat[0]])]
    )
    product = lax.dot_general(
        stacked, misfit, (((1, 3), (0, 2)), ((), ())), preferred_element_type=jnp.float32
    )
    product = product.reshape(2, K, P_SIZE, S)
    pull_real = jnp.sum(beam_float[0] * product[0] + beam_float[1] * product[1], axis=1)
    pull_imag = jnp.sum(beam_float[0] * product[1] - beam_float[1] * product[0], axis=1)
    shaped = seeded_flat.reshape(2, K, P_SIZE, S)
    gram_real = jnp.einsum(
        "kjq,kiq->kji", shaped[0], shaped[0], preferred_element_type=jnp.float32
    ) + jnp.einsum("kjq,kiq->kji", shaped[1], shaped[1], preferred_element_type=jnp.float32)
    gram_imag = jnp.einsum(
        "kjq,kiq->kji", shaped[0], shaped[1], preferred_element_type=jnp.float32
    ) - jnp.einsum("kjq,kiq->kji", shaped[1], shaped[0], preferred_element_type=jnp.float32)
    inner_real = jnp.einsum(
        "kji,kip->kjp", gram_real, beam_float[0], precision=highest
    ) + jnp.einsum("kji,kip->kjp", gram_imag, beam_float[1], precision=highest)
    inner_imag = jnp.einsum(
        "kji,kip->kjp", gram_imag, beam_float[0], precision=highest
    ) - jnp.einsum("kji,kip->kjp", gram_real, beam_float[1], precision=highest)
    denominator = jnp.sum(beam_float[0] * inner_real - beam_float[1] * inner_imag, axis=1)
    pull_real = pull_real + start_gains[0] * denominator
    pull_imag = pull_imag + start_gains[1] * denominator
    local_sums = jnp.stack([pull_real, pull_imag, denominator], axis=1)
    totals = lax.psum(local_sums, "tm")
    damped = update(totals, start_gains)
    mixed = jnp.einsum(
        "fg,gcks->fcks",
        blending,
        lax.all_to_all(damped[None], "freq", split_axis=3, concat_axis=0, tiled=True),
        precision=highest,
    )
    returned = lax.all_to_all(mixed, "freq", split_axis=0, concat_axis=3, tiled=True)
    smooth = returned[0]
    final = apply_gains(smooth, beam_float)
    residual = (observed_block.astype(jnp.float32) - predict(final)).astype(jnp.bfloat16)
    gains_out = lax.dynamic_slice_in_dim(smooth, lax.axis_index("tm") * owned, owned, 1)
    return (residual[None, None], gains_out[None])


def solution(mesh):
    return jax.shard_map(
        local,
        mesh=mesh,
        in_specs=(
            P("freq", "tm", None, None, None),
            P("freq", "tm", None, None, None),
            P(),
            P("freq", None, None, None),
            P(),
        ),
        out_specs=(P("freq", "tm", None, None, None), P("freq", None, "tm", None)),
        check_vma=False,
    )
```

profile of v0, /device:TPU:1, one launch (start us, length us, event | category | flops | bytes accessed | tf_op | source)
XLA Modules:
  0.0 244.0 jit_solution(8187503134172178200)
XLA Ops:
  7.2 0.7 compare_select_fusion
  7.9 0.7 compare_and_fusion
  8.6 1.6 copy.125
  10.4 1.7 gather_fusion
  12.1 1.0 broadcast_select_fusion
  13.2 0.1 fusion.24
  13.3 0.2 multiply_subtract_fusion.1
  13.6 0.2 fusion.38
  13.8 0.2 fusion.33
  14.0 0.7 fusion.58
  14.7 1.0 slice_bitcast_fusion.3
  15.8 0.2 convolution_add_fusion.1
  16.0 0.7 fusion.60
  16.7 0.2 convolution_subtract_fusion.1
  16.9 0.4 fusion.30
  17.3 0.4 fusion.28
  17.7 1.8 copy.88
  19.5 1.8 copy.87
  21.2 1.0 copy.89
  22.3 1.9 maximum_bitcast_fusion.2
  24.2 1.1 maximum_bitcast_fusion
  25.3 4.1 %convolution_bitcast_fusion = f32[2,256,512]{2,1,0:T(8,128)} fusion(bf16[1,2,256,512]{3,2,1,0:T(8,128)(2,1)} %get-tuple-element.19, bf16[1,2,256,512]{3,2,1,0:T(8,128)(2,1)} %get-tuple-element.18, bf16[512,512,1]{1,0,2:T(8,128)(2,1)S(1)} %bitcast.168, bf16[1,512,512]{1,2,0:T(8,128)(2,1)} %maximum_bitcast_fusion.2, bf16[1,512,512]{1,2,0:T(8,128)(2,1)} %copy.89, ...), kind=kOutput, calls=%fused_computation.7 | convolution fusion | flops 1076363264 | bytes 4718592 | tf_op jit(solution)/shard_map/dot_general | solution.py:48
  29.4 1.7 fusion.21
  31.1 0.4 fusion.6
  31.4 0.5 fusion.7
  32.0 0.7 pad_maximum_fusion
  32.7 150.6 %all-reduce.2.cloned.1.call-done = f32[32,3,512]{2,0,1:T(8,128)} async-done(((f32[32,3,512]{2,0,1:T(8,128)}), f32[32,3,512]{2,0,1:T(8,128)}) %all-reduce.2.cloned.1.call-update) | async-done | bytes 196624 | tf_op jit(solution)/shard_map/psum | solution.py:71
  183.3 0.9 slice_bitcast_fusion.6
  184.3 0.2 copy.90
  184.5 0.5 reshape.177
  185.0 28.3 %all_to_all.33 = f32[32,1,1024]{2,1,0:T(1,128)S(1)} all-to-all(f32[32,1,1024]{2,1,0:T(1,128)S(1)} %reshape.177), channel_id=1, replica_groups=mesh['freq'=32,'tm'=16] {'freq'}, dimensions={0} | all-to-all | bytes 262144 | tf_op jit(solution)/shard_map/all_to_all | solution.py:76
  213.3 0.5 broadcast.24
  213.8 0.9 reduce
  214.8 0.4 reshape.178
  215.2 0.3 copy.92
  215.6 0.6 convolution_bitcast_fusion.1
  216.2 0.5 copy.93
  216.6 0.9 reshape.179
  217.5 4.0 %all-to-all-start.1 = ((f32[32,1,1024]{2,1,0:T(1,128)}), f32[32,1,1024]{2,1,0:T(1,128)S(1)}, u32[]{:S(2)}, u32[]{:S(2)}) async-start(f32[32,1,1024]{2,1,0:T(1,128)} %reshape.179), calls=%async_computation.1 | async-start | bytes 262144 | tf_op jit(solution)/shard_map/all_to_all | solution.py:79
  221.5 9.4 %all-to-all-done.1 = f32[32,1,1024]{2,1,0:T(1,128)S(1)} async-done(((f32[32,1,1024]{2,1,0:T(1,128)}), f32[32,1,1024]{2,1,0:T(1,128)S(1)}, u32[]{:S(2)}, u32[]{:S(2)}) %all-to-all-start.1) | async-done | bytes 131104 | tf_op jit(solution)/shard_map/all_to_all | solution.py:79
  230.9 1.0 reduce.1
  231.9 0.2 reshape.180
  232.4 0.2 multiply_subtract_fusion
  233.0 0.2 copy.98
  233.2 0.2 constant_dynamic-slice_fusion
  233.4 0.8 copy.100
  234.3 1.2 copy-done.5
  235.4 1.7 fusion.2
  (29 shorter events, 1.0 us)
Async XLA Ops:
  7.2 208.4 %copy-start = (f32[32,32]{1,0:T(8,128)S(1)}, f32[32,32]{1,0:T(8,128)}, u32[]{:S(2)}) copy-start(f32[32,32]{1,0:T(8,128)} %param.9) | copy-start | bytes 12292
  7.2 3.1 %copy-start.1 = (f32[1,2,32,512]{3,2,1,0:T(8,128)S(1)}, f32[1,2,32,512]{3,2,1,0:T(8,128)}, u32[]{:S(2)}) copy-start(f32[1,2,32,512]{3,2,1,0:T(8,128)} %param.8) | copy-start | bytes 393220
  7.2 176.1 %all-reduce.2.cloned.1.call-start = ((), (), s32[]{:S(2)}) async-start(), calls=%async_computation.2 | async-start | bytes 393216 | tf_op jit(solution)/shard_map/psum | solution.py:71
  22.3 1.9 copy-start.2
  22.3 1.9 copy-start.3
  22.3 1.9 copy-start.4
  217.5 13.4 %all-to-all-start.1 = ((f32[32,1,1024]{2,1,0:T(1,128)}), f32[32,1,1024]{2,1,0:T(1,128)S(1)}, u32[]{:S(2)}, u32[]{:S(2)}) async-start(f32[32,1,1024]{2,1,0:T(1,128)} %reshape.179), calls=%async_computation.1 | async-start | bytes 262144 | tf_op jit(solution)/shard_map/all_to_all | solution.py:79
  234.2 1.2 copy-start.5
Sparse Core Ops, SparseCore 0:
  32.8 150.4 all-reduce.1
where the time goes:
time: 244 us
  waiting for transfers between devices  160 us (66%)
  blocking collectives  28.3 us (12%)
  local copies, waits for them, and re-layouts  16.3 us (7%)
  between operations  14.3 us (6%)
  other arithmetic  12.3 us (5%)
  matrix products  8.76 us (4%)
  starting transfers between devices  4 us (2%)
    psum x1, waiting for transfers between devices, local(): totals = lax.psum(local_sums, 'tm')  151 us
    all_to_all x1, blocking collectives, local(): lax.all_to_all(damped[None], 'freq', split_axis=3, concat_axis=0, tiled=T...  28.3 us
    all_to_all x1, waiting for transfers between devices, local(): lax.all_to_all(mixed, 'freq', split_axis=0, concat_axis=3, tiled=True)  9.43 us
  transfers between devices with their start and end apart: 2, of which 2 were waited for; matrix products, arithmetic and copies ran while one was open for 0% of the time, Pallas kernels for 0%

commit v1 on v0

--- a/solution.py
+++ b/solution.py
@@ -73,7 +73,12 @@
     mixed = jnp.einsum(
         "fg,gcks->fcks",
         blending,
-        lax.all_to_all(damped[None], "freq", split_axis=3, concat_axis=0, tiled=True),
+        jnp.concatenate(
+            lax.all_to_all(
+                jnp.stack(jnp.split(damped[None], lax.axis_size("freq"), axis=3)), "freq", 0, 0
+            ),
+            axis=0,
+        ),
         precision=highest,
     )
     returned = lax.all_to_all(mixed, "freq", split_axis=0, concat_axis=3, tiled=True)

time: 244 us -> 241 us (0.988)
  other arithmetic: 12.3 us -> 7.53 us
where the time goes in v1:
time: 241 us; the launch traced here: 240 us
  waiting for transfers between devices  160 us (66%)
  blocking collectives  28.3 us (12%)
  local copies, waits for them, and re-layouts  15.3 us (6%)
  between operations  14.7 us (6%)
  matrix products  10.3 us (4%)
  other arithmetic  7.53 us (3%)
  starting transfers between devices  4.18 us (2%)
    psum x1, waiting for transfers between devices, local(): totals = lax.psum(local_sums, 'tm')  150 us
    all_to_all x1, blocking collectives, local(): lax.all_to_all(jnp.stack(jnp.split(damped[None], lax.axis_size('freq'), a...  28.3 us
    all_to_all x1, waiting for transfers between devices, local(): lax.all_to_all(mixed, 'freq', split_axis=0, concat_axis=3, tiled=True)  9.43 us
  transfers between devices with their start and end apart: 2, of which 2 were waited for; matrix products, arithmetic and copies ran while one was open for 0% of the time, Pallas kernels for 0%

profile of v1, /device:TPU:1, one launch (start us, length us, event | category | flops | bytes accessed | tf_op | source)
XLA Modules:
  0.0 240.2 jit_solution(7628949097487826763)
XLA Ops:
  7.2 0.7 compare_select_fusion
  8.0 0.7 compare_and_fusion
  8.6 1.6 copy.1651
  10.3 0.7 fusion.62
  11.0 1.7 gather_fusion
  12.9 0.2 multiply_subtract_fusion.1
  13.3 0.9 fusion.41
  14.2 1.0 broadcast_select_fusion
  15.2 0.9 fusion.36
  16.1 1.0 copy.1602
  17.1 1.0 copy.1603
  18.1 1.1 maximum_bitcast_fusion
  19.2 3.1 %convolution_bitcast_fusion = f32[2,256,512]{2,1,0:T(8,128)S(1)} fusion(bf16[1,2,256,512]{3,2,1,0:T(8,128)(2,1)} %get-tuple-element.21, bf16[1,2,256,512]{3,2,1,0:T(8,128)(2,1)} %get-tuple-element.20, bf16[512,512,1]{1,0,2:T(8,128)(2,1)S(1)} %bitcast.286, bf16[1,512,512]{1,2,0:T(8,128)(2,1)} %bitcast.304, bf16[1,512,512]{1,2,0:T(8,128)(2,1)} %copy.1603, ...), kind=kOutput, calls=%fused_computation.7 | convolution fusion | flops 1076363264 | bytes 4718592 | tf_op jit(solution)/shard_map/dot_general | solution.py:48
  22.3 0.5 fusion.23
  23.2 0.2 convolution_add_fusion.1
  23.4 0.7 fusion.60
  24.3 0.2 convolution_subtract_fusion.1
  24.5 0.4 fusion.32
  24.9 0.4 fusion.30
  25.3 0.4 fusion.6
  25.7 0.5 fusion.7
  26.3 0.2 copy-done.3
  27.2 0.7 pad_maximum_fusion.2
  27.9 0.2 copy.1615
  28.1 150.4 %all-reduce.2.cloned.1.call-done = f32[32,3,512]{2,0,1:T(8,128)} async-done(((f32[32,3,512]{2,0,1:T(8,128)}), f32[32,3,512]{2,0,1:T(8,128)}) %all-reduce.2.cloned.1.call-update) | async-done | bytes 196624 | tf_op jit(solution)/shard_map/psum | solution.py:71
  178.5 0.9 fusion.61
  180.3 0.3 reshape.181
  180.6 28.3 %all_to_all.20 = f32[32,1,1024]{2,1,0:T(1,128)S(1)} all-to-all(f32[32,1,1024]{2,1,0:T(1,128)S(1)} %reshape.181), channel_id=1, replica_groups=mesh['freq'=32,'tm'=16] {'freq'}, dimensions={0} | all-to-all | bytes 262144 | tf_op jit(solution)/shard_map/all_to_all | solution.py:77
  208.8 0.5 broadcast.24
  209.3 0.9 reduce
  210.3 0.2 reshape.182
  210.5 0.3 copy.1616
  210.8 0.6 convolution_bitcast_fusion.1
  211.4 0.5 copy.1617
  211.8 0.9 reshape.183
  212.8 4.1 %all-to-all-start.1 = ((f32[32,1,1024]{2,1,0:T(1,128)}), f32[32,1,1024]{2,1,0:T(1,128)S(1)}, u32[]{:S(2)}, u32[]{:S(2)}) async-start(f32[32,1,1024]{2,1,0:T(1,128)} %reshape.183), calls=%async_computation.1 | async-start | bytes 262144 | tf_op jit(solution)/shard_map/all_to_all | solution.py:84
  216.9 9.4 %all-to-all-done.1 = f32[32,1,1024]{2,1,0:T(1,128)S(1)} async-done(((f32[32,1,1024]{2,1,0:T(1,128)}), f32[32,1,1024]{2,1,0:T(1,128)S(1)}, u32[]{:S(2)}, u32[]{:S(2)}) %all-to-all-start.1) | async-done | bytes 131104 | tf_op jit(solution)/shard_map/all_to_all | solution.py:84
  226.3 1.0 reduce.1
  227.3 0.2 reshape.184
  227.5 0.3 copy.1618
  227.8 0.3 copy.1625
  228.4 0.2 copy.1621
  228.7 0.2 multiply_subtract_fusion
  229.0 0.2 copy.1623
  229.2 0.2 copy.1624
  229.5 0.2 constant_dynamic-slice_fusion
  229.7 0.8 copy.1626
  230.4 2.9 %fusion.2 = bf16[1,1,2,512,512]{4,3,2,1,0:T(8,128)(2,1)} fusion(bf16[512,512,1]{1,0,2:T(8,128)(2,1)S(1)} %bitcast.289, bf16[1,512,512]{1,2,0:T(8,128)(2,1)S(1)} %bitcast.305, bf16[1,512,512]{1,2,0:T(8,128)(2,1)S(1)} %copy.1624, bf16[1,1,2,512,512]{4,3,2,1,0:T(8,128)(2,1)} %param.5), kind=kOutput, calls=%fused_computation.5 | convolution fusion | flops 538968064 | bytes 3670016 | tf_op jit(solution)/shard_map/dot_general | solution.py:22
  (76 shorter events, 2.9 us)
Async XLA Ops:
  7.2 203.6 %copy-start = (f32[32,32]{1,0:T(8,128)S(1)}, f32[32,32]{1,0:T(8,128)}, u32[]{:S(2)}) copy-start(f32[32,32]{1,0:T(8,128)} %param.9) | copy-start | bytes 12292
  7.2 3.2 %copy-start.1 = (f32[1,2,32,512]{3,2,1,0:T(8,128)S(1)}, f32[1,2,32,512]{3,2,1,0:T(8,128)}, u32[]{:S(2)}) copy-start(f32[1,2,32,512]{3,2,1,0:T(8,128)} %param.8) | copy-start | bytes 393220
  7.2 171.3 %all-reduce.2.cloned.1.call-start = ((), (), s32[]{:S(2)}) async-start(), calls=%async_computation.2 | async-start | bytes 393216 | tf_op jit(solution)/shard_map/psum | solution.py:71
  8.6 1.6 copy-start.6
  13.2 1.0 copy-start.7
  22.3 0.9 copy-start.5
  23.4 0.9 copy-start.4
  25.7 0.8 copy-start.3
  25.7 1.0 copy-start.2
  212.8 13.6 %all-to-all-start.1 = ((f32[32,1,1024]{2,1,0:T(1,128)}), f32[32,1,1024]{2,1,0:T(1,128)S(1)}, u32[]{:S(2)}, u32[]{:S(2)}) async-start(f32[32,1,1024]{2,1,0:T(1,128)} %reshape.183), calls=%async_computation.1 | async-start | bytes 262144 | tf_op jit(solution)/shard_map/all_to_all | solution.py:84
Sparse Core Ops, SparseCore 0:
  28.0 150.4 all-reduce.1

commit v2 on v0

--- a/solution.py
+++ b/solution.py
@@ -68,7 +68,7 @@
     pull_real = pull_real + start_gains[0] * denominator
     pull_imag = pull_imag + start_gains[1] * denominator
     local_sums = jnp.stack([pull_real, pull_imag, denominator], axis=1)
-    totals = lax.psum(local_sums, "tm")
+    totals = jnp.sum(lax.all_gather(local_sums, "tm"), axis=0)
     damped = update(totals, start_gains)
     mixed = jnp.einsum(
         "fg,gcks->fcks",

time: 244 us -> 190 us (0.78)
  waiting for transfers between devices: 160 us -> 109 us
  blocking collectives: 28.3 us -> 20.8 us
  other arithmetic: 12.3 us -> 15.6 us
    psum x1 -> x0, waiting for transfers between devices: 151 us -> none  [local(): totals = lax.psum(local_sums, 'tm')]
    all_gather x0 -> x1, waiting for transfers between devices: none -> 99.8 us  [local(): totals = jnp.sum(lax.all_gather(local_sums, 'tm'), axis=0)]
    all_to_all x1, blocking collectives: 28.3 us -> 20.8 us  [local(): lax.all_to_all(damped[None], 'freq', split_axis=3, concat_axis=0, tiled=T...]
where the time goes in v2:
time: 190 us; the launch traced here: 189 us
  waiting for transfers between devices  109 us (57%)
  blocking collectives  20.8 us (11%)
  other arithmetic  15.6 us (8%)
  local copies, waits for them, and re-layouts  15.1 us (8%)
  between operations  14.3 us (8%)
  matrix products  10 us (5%)
  starting transfers between devices  4.18 us (2%)
    all_gather x1, waiting for transfers between devices, local(): totals = jnp.sum(lax.all_gather(local_sums, 'tm'), axis=0)  99.8 us
    all_to_all x1, blocking collectives, local(): lax.all_to_all(damped[None], 'freq', split_axis=3, concat_axis=0, tiled=T...  20.8 us
    all_to_all x1, waiting for transfers between devices, local(): lax.all_to_all(mixed, 'freq', split_axis=0, concat_axis=3, tiled=True)  9.43 us
    all_to_all x1, starting transfers between devices, local(): lax.all_to_all(mixed, 'freq', split_axis=0, concat_axis=3, tiled=True)  4.14 us
    dot_general x1, matrix products, local(): lax.dot_general(stacked, misfit, (((1, 3), (0, 2)), ((), ())), preferred_...  4.08 us
  transfers between devices with their start and end apart: 2, of which 2 were waited for; matrix products, arithmetic and copies ran while one was open for 0% of the time, Pallas kernels for 0%

profile of v2, /device:TPU:1, one launch (start us, length us, event | category | flops | bytes accessed | tf_op | source)
XLA Modules:
  0.0 189.2 jit_solution(3832061681936220256)
XLA Ops:
  7.2 0.7 compare_select_fusion
  7.9 0.7 compare_and_fusion
  8.6 1.6 copy.113
  10.3 0.9 slice_bitcast_fusion.10
  11.2 1.7 gather_fusion
  12.9 1.0 broadcast_select_fusion
  14.0 0.1 fusion.24
  14.1 0.2 multiply_subtract_fusion.1
  14.4 0.2 fusion.38
  14.6 0.2 fusion.33
  14.8 0.7 fusion.58
  15.6 1.0 slice_bitcast_fusion.3
  16.6 0.2 convolution_add_fusion.1
  16.8 0.7 fusion.60
  17.5 0.2 convolution_subtract_fusion.1
  17.8 0.4 fusion.30
  18.1 0.4 fusion.28
  18.5 1.8 copy.76
  20.3 1.8 copy.75
  22.1 1.0 copy.77
  23.1 1.8 maximum_bitcast_fusion.2
  25.0 2.3 %maximum_bitcast_fusion = (bf16[1,2,256,512]{3,2,1,0:T(8,128)(2,1)}, bf16[1,2,256,512]{3,2,1,0:T(8,128)(2,1)}) fusion(bf16[1,256,512]{2,1,0:T(8,128)(2,1)} %fusion.58, bf16[1,256,512]{2,1,0:T(8,128)(2,1)} %get-tuple-element.15, bf16[1,256,512]{2,1,0:T(8,128)(2,1)} %get-tuple-element.14), kind=kLoop, calls=%fused_computation.31 | loop fusion | flops 524288 | bytes 1835008 | tf_op jit(solution)/shard_map/stack | solution.py:45
  27.3 4.1 %convolution_bitcast_fusion = f32[2,256,512]{2,1,0:T(8,128)} fusion(bf16[1,2,256,512]{3,2,1,0:T(8,128)(2,1)} %get-tuple-element.19, bf16[1,2,256,512]{3,2,1,0:T(8,128)(2,1)} %get-tuple-element.18, bf16[512,512,1]{1,0,2:T(8,128)(2,1)S(1)} %bitcast.169, bf16[1,512,512]{1,2,0:T(8,128)(2,1)} %maximum_bitcast_fusion.2, bf16[1,512,512]{1,2,0:T(8,128)(2,1)} %copy.77, ...), kind=kOutput, calls=%fused_computation.7 | convolution fusion | flops 1076363264 | bytes 4718592 | tf_op jit(solution)/shard_map/dot_general | solution.py:48
  31.4 1.7 fusion.21
  33.1 0.4 fusion.6
  33.4 0.5 fusion.7
  34.0 0.7 pad_maximum_fusion
  34.7 99.8 %all-gather.3.cloned.1.call-done = f32[512,3,512]{2,0,1:T(8,128)} async-done(((f32[32,3,512]{2,0,1:T(8,128)}), f32[512,3,512]{2,0,1:T(8,128)}) %all-gather.3.cloned.1.call-update) | async-done | bytes 3145744 | tf_op jit(solution)/shard_map/all_gather | solution.py:71
  134.5 2.2 %reduce_sum.48 = f32[32,3,512]{2,0,1:T(8,128)S(1)} reduce(f32[16,32,3,512]{3,1,0,2:T(8,128)} %bitcast.173, f32[]{:T(128)} %constant.7.clone.1), dimensions={0}, to_apply=%region_3.4 | reduce | flops 737280 | bytes 3342340 | tf_op jit(solution)/shard_map/reduce_sum | solution.py:71
  136.7 0.2 copy.78
  137.0 0.5 reshape.178
  137.5 20.8 %all_to_all.33 = f32[32,1,1024]{2,1,0:T(1,128)S(1)} all-to-all(f32[32,1,1024]{2,1,0:T(1,128)S(1)} %reshape.178), channel_id=1, replica_groups=mesh['freq'=32,'tm'=16] {'freq'}, dimensions={0} | all-to-all | bytes 262144 | tf_op jit(solution)/shard_map/all_to_all | solution.py:76
  158.3 0.5 broadcast.24
  158.9 0.9 reduce
  159.8 0.4 reshape.179
  160.3 0.3 copy.80
  160.6 0.6 convolution_bitcast_fusion.1
  161.2 0.5 copy.81
  161.6 0.9 reshape.180
  162.6 4.1 %all-to-all-start.1 = ((f32[32,1,1024]{2,1,0:T(1,128)}), f32[32,1,1024]{2,1,0:T(1,128)S(1)}, u32[]{:S(2)}, u32[]{:S(2)}) async-start(f32[32,1,1024]{2,1,0:T(1,128)} %reshape.180), calls=%async_computation.1 | async-start | bytes 262144 | tf_op jit(solution)/shard_map/all_to_all | solution.py:79
  166.7 9.4 %all-to-all-done.1 = f32[32,1,1024]{2,1,0:T(1,128)S(1)} async-done(((f32[32,1,1024]{2,1,0:T(1,128)}), f32[32,1,1024]{2,1,0:T(1,128)S(1)}, u32[]{:S(2)}, u32[]{:S(2)}) %all-to-all-start.1) | async-done | bytes 131104 | tf_op jit(solution)/shard_map/all_to_all | solution.py:79
  176.1 1.0 reduce.1
  177.1 0.2 reshape.181
  177.6 0.2 multiply_subtract_fusion
  178.2 0.2 copy.86
  178.4 0.2 constant_dynamic-slice_fusion
  178.6 0.8 copy.88
  179.5 2.9 %fusion.2 = bf16[1,1,2,512,512]{4,3,2,1,0:T(8,128)(2,1)} fusion(bf16[512,512,1]{1,0,2:T(8,128)(2,1)S(1)} %bitcast.172, bf16[1,512,512]{1,2,0:T(8,128)(2,1)S(1)} %maximum_bitcast_fusion.3, bf16[1,512,512]{1,2,0:T(8,128)(2,1)S(1)} %copy.86, bf16[1,1,2,512,512]{4,3,2,1,0:T(8,128)(2,1)} %param.5), kind=kOutput, calls=%fused_computation.5 | convolution fusion | flops 538968064 | bytes 3670016 | tf_op jit(solution)/shard_map/dot_general | solution.py:22
  (22 shorter events, 1.0 us)
Async XLA Ops:
  7.2 153.4 %copy-start = (f32[32,32]{1,0:T(8,128)S(1)}, f32[32,32]{1,0:T(8,128)}, u32[]{:S(2)}) copy-start(f32[32,32]{1,0:T(8,128)} %param.9) | copy-start | bytes 12292
  7.2 127.3 %all-gather.3.cloned.1.call-start = ((), (), s32[]{:S(2)}) async-start(), calls=%async_computation.2 | async-start | bytes 3342336 | tf_op jit(solution)/shard_map/all_gather | solution.py:71
  33.0 0.9 copy-start.1
  162.6 13.6 %all-to-all-start.1 = ((f32[32,1,1024]{2,1,0:T(1,128)}), f32[32,1,1024]{2,1,0:T(1,128)S(1)}, u32[]{:S(2)}, u32[]{:S(2)}) async-start(f32[32,1,1024]{2,1,0:T(1,128)} %reshape.180), calls=%async_computation.1 | async-start | bytes 262144 | tf_op jit(solution)/shard_map/all_to_all | solution.py:79
Sparse Core Ops, SparseCore 0:
  34.8 99.6 all-gather.2
